TPU v7x, 256 devices: a whole 4x4x8 slice. The times are simulated.
256 devices in a mesh: row: 16 (over x_hi, y, core), col: 16 (over z, x_lo).
Axes of the slice: x: 4 (x_hi: 2, x_lo: 2; x = x_hi * 2 + x_lo), y: 4, z: 8, core: 2. Of those that a mesh axis runs over, the one named last changes fastest.
Arguments:
- vectors: float32 [16, 32768], P(None, ('col', 'row')), may hold values from -6 to 6
- tile_blocks: float32 [16, 16, 128, 128, 128], P('row', 'col'), may hold values from -0.046875 to 0.046875
- coords: int32 [16, 16, 128], P('row', 'col'), may hold values from 0 to 255, as said below
- counts: int32 [16, 16], P('row', 'col'), may hold values from 1 to 128, as said below
Outputs:
- product: float32 [16, 32768], P(None, ('col', 'row'))
Inputs may be any that keep to these rules, and one draw needn't show every extreme that they name: `counts`: every cell has at least one live slot and some cell has exactly 128. `coords`: within one cell all 128 entries are distinct; slots at or past counts hold no tile of S.
All inputs are finite; a program needn't handle non-finite values.
Results may differ from a plain program's by a relative error of at most 0.0003.
Values sent between devices are 32-bit elements; how exact they have to be, the bound alone decides.
No kernel may reach another device: no remote copies, remote signals or barrier semaphores. Data moves between devices by JAX's collectives and lax.ppermute only.
A program may use at most 64 MiB of HBM per device.

v0:
```python
import jax
import jax.numpy as jnp
from jax import lax
from jax.sharding import PartitionSpec as P

HIGH = lax.Precision.HIGHEST


def from_root(value, axis, source):
    kept = jnp.where(lax.axis_index(axis) == source, value, 0).astype(value.dtype)
    return lax.psum(kept, axis)


def slot_terms(blocks, slot_coords, live_mask, x_col, x_row):
    vec_count = x_col.shape[0]
    tile_size = blocks.shape[-1]
    seg_tiles = x_row.shape[1] // tile_size
    col_tiles = x_col.shape[1] // tile_size
    row_pos = slot_coords // col_tiles
    col_pos = slot_coords % col_tiles
    picked_col = jnp.take(x_col.reshape(vec_count, col_tiles, tile_size), col_pos, axis=1)
    picked_row = jnp.take(x_row.reshape(vec_count, seg_tiles, tile_size), row_pos, axis=1)
    normal = jnp.einsum("vsk,smk->vsm", picked_col, blocks, precision=HIGH)
    transposed = jnp.einsum("vsm,smk->vsk", picked_row, blocks, precision=HIGH)
    onehot_rows = (row_pos[:, None] == jnp.arange(seg_tiles, dtype=jnp.int32)[None, :]).astype(
        jnp.float32
    ) * live_mask[:, None]
    onehot_cols = (col_pos[:, None] == jnp.arange(col_tiles, dtype=jnp.int32)[None, :]).astype(
        jnp.float32
    ) * live_mask[:, None]
    row_terms = jnp.einsum("st,vsm->vtm", onehot_rows, normal, precision=HIGH).reshape(
        vec_count, seg_tiles * tile_size
    )
    col_terms = jnp.einsum("st,vsk->vtk", onehot_cols, transposed, precision=HIGH).reshape(
        vec_count, col_tiles * tile_size
    )
    return (row_terms, col_terms)


def local(vectors, tile_blocks, coords, counts):
    n_row = lax.axis_size("row")
    n_col = lax.axis_size("col")
    seg_ratio = n_row // n_col
    max_slots = tile_blocks.shape[2]
    tile_size = tile_blocks.shape[-1]
    blocks = tile_blocks.reshape(max_slots, tile_size, tile_size)
    slot_coords = coords.reshape(max_slots)
    slot_count = counts.reshape(())
    row_idx = lax.axis_index("row")
    col_idx = lax.axis_index("col")
    x_col = lax.all_gather(vectors, "row", axis=1, tiled=True)
    x_row = from_root(x_col, "col", row_idx // seg_ratio)
    live_mask = (jnp.arange(max_slots, dtype=jnp.int32) < slot_count).astype(jnp.float32)
    row_terms, col_terms = slot_terms(blocks, slot_coords, live_mask, x_col, x_row)
    whole_row = lax.psum(row_terms, "col")
    is_owner = (col_idx == row_idx // seg_ratio).astype(jnp.float32)
    placed = whole_row * is_owner
    return lax.psum_scatter(col_terms + placed, "row", scatter_dimension=1, tiled=True)


def solution(mesh):
    return jax.shard_map(
        local,
        mesh=mesh,
        in_specs=(
            P(None, ("col", "row")),
            P("row", "col", None, None, None),
            P("row", "col", None),
            P("row", "col"),
        ),
        out_specs=P(None, ("col", "row")),
        check_vma=False,
    )
```

profile of v0, /device:TPU:32, one launch (start us, length us, event | category | flops | bytes accessed | tf_op | source)
XLA Modules:
  0.0 276.1 jit_solution(18044098846579297185)
XLA Ops:
  6.5 0.0 all-reduce.3.cloned.1.call-start
  7.2 0.7 compare_and_fusion.1
  7.9 25.0 %all_gather.3 = f32[16,2048]{1,0:T(8,128)S(1)} all-gather(f32[16,128]{1,0:T(8,128)} %param.6), channel_id=1, replica_groups=mesh['row'=16,'col'=16] {'row'}, dimensions={1}, use_global_device_ids=true | all-gather | bytes 139264 | tf_op jit(solution)/shard_map/all_gather | solution.py:51
  32.9 0.8 gather_fusion.1
  33.7 15.5 %fusion.7 = f32[16,128,128]{2,0,1:T(8,128)S(1)} fusion(f32[1,1,128,128,128]{4,3,2,1,0:T(8,128)} %param.7, f32[128,16,128]{2,1,0:T(8,128)S(1)} %gather_fusion.1, pred[128]{0:T(512)(128)(4,1)S(1)} %get-tuple-element.12), kind=kOutput, calls=%fused_computation.7 | convolution fusion | flops 402915328 | bytes 10485888 | tf_op jit(solution)/shard_map/vsk,smk->vsm/dot_general | solution.py:23
  49.1 0.9 fusion.12
  50.1 0.7 copy.21
  50.8 0.7 copy_bitcast_fusion.2
  51.4 0.0 all-reduce.3.cloned.1.call-update
  51.5 0.0 reduce-scatter.2.cloned.1.call-start
  51.5 134.0 %all-reduce.3.cloned.1.call-done = (f32[16,16,128]{2,0,1:T(8,128)}, f32[16,2048]{1,0:T(8,128)}) async-done(((f32[16,16,128]{2,0,1:T(8,128)}, f32[16,2048]{1,0:T(8,128)}), (f32[16,16,128]{2,0,1:T(8,128)}, f32[16,2048]{1,0:T(8,128)})) %all-reduce.3.cloned.1.call-update) | async-done | bytes 262160 | tf_op jit(solution)/shard_map/psum | solution.py:11
  185.5 0.0 copy-start
  185.6 1.6 gather_fusion
  187.1 9.6 %fusion.4 = f32[16,128,128]{2,0,1:T(8,128)S(1)} fusion(f32[1,1,128,128,128]{4,3,2,1,0:T(8,128)} %param.7, f32[128,16,128]{2,1,0:T(8,128)S(1)} %gather_fusion, pred[128]{0:T(512)(128)(4,1)S(1)} %get-tuple-element.8), kind=kOutput, calls=%fused_computation.6 | convolution fusion | flops 402915328 | bytes 10485888 | tf_op jit(solution)/shard_map/vsm,smk->vsk/dot_general | solution.py:24
  196.8 0.9 fusion.14
  197.7 0.0 copy-done
  197.7 0.7 bitcast_add_fusion
  198.4 0.0 reduce-scatter.2.cloned.1.call-update
  198.4 70.9 %reduce-scatter.2.cloned.1.call-done = f32[16,128]{1,0:T(8,128)} async-done(((f32[16,2048]{1,0:T(8,128)}), f32[16,128]{1,0:T(8,128)}) %reduce-scatter.2.cloned.1.call-update) | async-done | bytes 8208 | tf_op jit(solution)/shard_map/reduce_scatter | solution.py:58
  (5 shorter events, 0.0 us)
Async XLA Ops:
  6.5 179.0 %all-reduce.3.cloned.1.call-start = ((), (), s32[]{:S(2)}) async-start(), calls=%async_computation.2 | async-start | bytes 524288 | tf_op jit(solution)/shard_map/psum | solution.py:11
  51.5 217.9 %reduce-scatter.2.cloned.1.call-start = ((), (), s32[]{:S(2)}) async-start(), calls=%async_computation.1 | async-start | bytes 139264 | tf_op jit(solution)/shard_map/reduce_scatter | solution.py:58
  185.5 12.1 %copy-start = (f32[16,2048]{1,0:T(8,128)S(1)}, f32[16,2048]{1,0:T(8,128)}, u32[]{:S(2)}) copy-start(f32[16,2048]{1,0:T(8,128)} %get-tuple-element.7) | copy-start | bytes 393220
Sparse Core Ops, SparseCore 0:
  51.6 133.9 all-reduce.2
  198.5 70.7 reduce-scatter.1
where the time goes:
time: 276 us
  waiting for transfers between devices  205 us (74%)
  matrix products  26.9 us (10%)
  blocking collectives  25 us (9%)
  between operations  14.1 us (5%)
  local copies, waits for them, and re-layouts  3.07 us (1%)
    psum x1, waiting for transfers between devices, from_root(): return lax.psum(kept, axis)  134 us
    reduce_scatter x1, waiting for transfers between devices, local(): lax.psum_scatter(col_terms + placed, 'row', scatter_dimension=1, tiled=True)  70.9 us
    all_gather x1, blocking collectives, local(): x_col = lax.all_gather(vectors, 'row', axis=1, tiled=True)  25 us
    dot_general x1, matrix products, slot_terms(): normal = jnp.einsum('vsk,smk->vsm', picked_col, blocks, precision=HIGH)  15.5 us
    dot_general x1, matrix products, slot_terms(): transposed = jnp.einsum('vsm,smk->vsk', picked_row, blocks, precision=HIGH)  9.6 us
  transfers between devices with their start and end apart: 2, of which 2 were waited for; matrix products, arithmetic and copies ran while one was open for 0% of the time, Pallas kernels for 0%

commit v1 on v0

--- a/solution.py
+++ b/solution.py
@@ -48,7 +48,9 @@
     slot_count = counts.reshape(())
     row_idx = lax.axis_index("row")
     col_idx = lax.axis_index("col")
-    x_col = lax.all_gather(vectors, "row", axis=1, tiled=True)
+    x_col = jnp.concatenate(
+        lax.all_to_all(jnp.stack([vectors] * lax.axis_size("row")), "row", 0, 0), axis=1
+    )
     x_row = from_root(x_col, "col", row_idx // seg_ratio)
     live_mask = (jnp.arange(max_slots, dtype=jnp.int32) < slot_count).astype(jnp.float32)
     row_terms, col_terms = slot_terms(blocks, slot_coords, live_mask, x_col, x_row)

time: 276 us -> 267 us (0.967)
  blocking collectives: 25 us -> 0 us
  starting transfers between devices: 0.04 us -> 7.12 us
  waiting for transfers between devices: 205 us -> 212 us
    all_gather x1 -> x0, blocking collectives: 25 us -> none  [local(): x_col = lax.all_gather(vectors, 'row', axis=1, tiled=True)]
    all_to_all x0 -> x1, starting transfers between devices: none -> 7.03 us  [local(): lax.all_to_all(jnp.stack([vectors] * lax.axis_size('row')), 'row', 0, 0)]
    all_to_all x0 -> x1, waiting for transfers between devices: none -> 6.76 us  [local(): lax.all_to_all(jnp.stack([vectors] * lax.axis_size('row')), 'row', 0, 0)]
  transfers between devices with their start and end apart: 2 -> 3, of which waited for: 2 -> 3; matrix products, arithmetic and copies ran while one was open for 0% -> 0% of each run, Pallas kernels for 0% -> 0%
where the time goes in v1:
time: 267 us; the launch traced here: 266 us
  waiting for transfers between devices  212 us (79%)
  matrix products  26.9 us (10%)
  between operations  14.2 us (5%)
  starting transfers between devices  7.12 us (3%)
  local copies, waits for them, and re-layouts  4.39 us (2%)
    psum x1, waiting for transfers between devices, from_root(): return lax.psum(kept, axis)  134 us
    reduce_scatter x1, waiting for transfers between devices, local(): lax.psum_scatter(col_terms + placed, 'row', scatter_dimension=1, tiled=True)  70.9 us
    dot_general x1, matrix products, slot_terms(): normal = jnp.einsum('vsk,smk->vsm', picked_col, blocks, precision=HIGH)  15.5 us
    dot_general x1, matrix products, slot_terms(): transposed = jnp.einsum('vsm,smk->vsk', picked_row, blocks, precision=HIGH)  9.6 us
    all_to_all x1, starting transfers between devices, local(): lax.all_to_all(jnp.stack([vectors] * lax.axis_size('row')), 'row', 0, 0)  7.03 us
    all_to_all x1, waiting for transfers between devices, local(): lax.all_to_all(jnp.stack([vectors] * lax.axis_size('row')), 'row', 0, 0)  6.76 us
  transfers between devices with their start and end apart: 3, of which 3 were waited for; matrix products, arithmetic and copies ran while one was open for 0% of the time, Pallas kernels for 0%

profile of v1, /device:TPU:32, one launch (start us, length us, event | category | flops | bytes accessed | tf_op | source)
XLA Modules:
  0.0 266.3 jit_solution(1790296000401507476)
XLA Ops:
  6.5 1.4 stack.2
  7.9 7.0 %all-to-all-start = ((f32[16,16,128]{2,1,0:T(8,128)}), f32[16,16,128]{2,1,0:T(8,128)S(1)}, u32[]{:S(2)}, u32[]{:S(2)}) async-start(f32[16,16,128]{2,1,0:T(8,128)} %stack.2), calls=%async_computation | async-start | bytes 262144 | tf_op jit(solution)/shard_map/all_to_all | solution.py:52
  14.9 0.0 all-reduce.3.cloned.1.call-start
  15.0 0.7 compare_and_fusion.1
  16.3 6.8 %all-to-all-done = f32[16,16,128]{2,1,0:T(8,128)S(1)} async-done(((f32[16,16,128]{2,1,0:T(8,128)}), f32[16,16,128]{2,1,0:T(8,128)S(1)}, u32[]{:S(2)}, u32[]{:S(2)}) %all-to-all-start) | async-done | bytes 131104 | tf_op jit(solution)/shard_map/all_to_all | solution.py:52
  23.1 0.8 gather_fusion.1
  23.9 15.5 %fusion = f32[128,16,128]{2,1,0:T(8,128)S(1)} fusion(f32[1,1,128,128,128]{4,3,2,1,0:T(8,128)} %param.7, f32[128,16,128]{2,1,0:T(8,128)S(1)} %gather_fusion.1, pred[128]{0:T(512)(128)(4,1)S(1)} %get-tuple-element.12), kind=kOutput, calls=%fused_computation.2 | convolution fusion | flops 402915328 | bytes 10485888 | tf_op jit(solution)/shard_map/vsk,smk->vsm/dot_general | solution.py:23
  39.3 0.9 fusion.4
  40.3 0.7 copy.19
  41.0 0.7 broadcast_select_fusion
  41.6 0.0 all-reduce.3.cloned.1.call-update
  41.6 0.0 reduce-scatter.2.cloned.1.call-start
  41.7 134.0 %all-reduce.3.cloned.1.call-done = (f32[16,16,128]{2,0,1:T(8,128)}, f32[16,2048]{1,0:T(8,128)}) async-done(((f32[16,16,128]{2,0,1:T(8,128)}, f32[16,2048]{1,0:T(8,128)}), (f32[16,16,128]{2,0,1:T(8,128)}, f32[16,2048]{1,0:T(8,128)})) %all-reduce.3.cloned.1.call-update) | async-done | bytes 262160 | tf_op jit(solution)/shard_map/psum | solution.py:11
  175.7 0.0 copy-start
  175.7 1.6 gather_fusion
  177.3 9.6 %fusion.2 = f32[128,16,128]{2,1,0:T(8,128)S(1)} fusion(f32[1,1,128,128,128]{4,3,2,1,0:T(8,128)} %param.7, f32[128,16,128]{2,1,0:T(8,128)S(1)} %gather_fusion, pred[128]{0:T(512)(128)(4,1)S(1)} %get-tuple-element.8), kind=kOutput, calls=%fused_computation.4 | convolution fusion | flops 402915328 | bytes 10485888 | tf_op jit(solution)/shard_map/vsm,smk->vsk/dot_general | solution.py:24
  186.9 0.9 fusion.7
  187.8 0.0 copy-done
  187.8 0.7 bitcast_add_fusion
  188.5 0.0 reduce-scatter.2.cloned.1.call-update
  188.5 70.9 %reduce-scatter.2.cloned.1.call-done = f32[16,128]{1,0:T(8,128)} async-done(((f32[16,2048]{1,0:T(8,128)}), f32[16,128]{1,0:T(8,128)}) %reduce-scatter.2.cloned.1.call-update) | async-done | bytes 8208 | tf_op jit(solution)/shard_map/reduce_scatter | solution.py:60
  (5 shorter events, 0.0 us)
Async XLA Ops:
  7.9 15.2 %all-to-all-start = ((f32[16,16,128]{2,1,0:T(8,128)}), f32[16,16,128]{2,1,0:T(8,128)S(1)}, u32[]{:S(2)}, u32[]{:S(2)}) async-start(f32[16,16,128]{2,1,0:T(8,128)} %stack.2), calls=%async_computation | async-start | bytes 262144 | tf_op jit(solution)/shard_map/all_to_all | solution.py:52
  14.9 160.7 %all-reduce.3.cloned.1.call-start = ((), (), s32[]{:S(2)}) async-start(), calls=%async_computation.3 | async-start | bytes 524288 | tf_op jit(solution)/shard_map/psum | solution.py:11
  41.6 217.8 %reduce-scatter.2.cloned.1.call-start = ((), (), s32[]{:S(2)}) async-start(), calls=%async_computation.2 | async-start | bytes 139264 | tf_op jit(solution)/shard_map/reduce_scatter | solution.py:60
  175.7 12.1 %copy-start = (f32[16,2048]{1,0:T(8,128)S(1)}, f32[16,2048]{1,0:T(8,128)}, u32[]{:S(2)}) copy-start(f32[16,2048]{1,0:T(8,128)} %get-tuple-element.7) | copy-start | bytes 393220
Sparse Core Ops, SparseCore 0:
  41.8 133.8 all-reduce.2
  188.7 70.7 reduce-scatter.1

commit v2 on v0

--- a/solution.py
+++ b/solution.py
@@ -8,7 +8,7 @@
 
 def from_root(value, axis, source):
     kept = jnp.where(lax.axis_index(axis) == source, value, 0).astype(value.dtype)
-    return lax.psum(kept, axis)
+    return jnp.sum(lax.all_gather(kept, axis), axis=0)
 
 
 def slot_terms(blocks, slot_coords, live_mask, x_col, x_row):

time: 276 us -> 320 us (1.16)
  waiting for transfers between devices: 205 us -> 247 us
    all_gather x0 -> x1, waiting for transfers between devices: none -> 49.6 us  [from_root(): return jnp.sum(lax.all_gather(kept, axis), axis=0)]
    psum x1, waiting for transfers between devices: 134 us -> 125 us  [local(): whole_row = lax.psum(row_terms, 'col')]
  transfers between devices with their start and end apart: 2 -> 3, of which waited for: 2 -> 3; matrix products, arithmetic and copies ran while one was open for 0% -> 10% of each run, Pallas kernels for 0% -> 0%
where the time goes in v2:
time: 320 us
  waiting for transfers between devices  247 us (77%)
  matrix products  26.9 us (8%)
  blocking collectives  25 us (8%)
  between operations  13.9 us (4%)
  other arithmetic  4.65 us (1%)
    psum x1, waiting for transfers between devices, local(): whole_row = lax.psum(row_terms, 'col')  125 us
    reduce_scatter x1, waiting for transfers between devices, local(): lax.psum_scatter(col_terms + placed, 'row', scatter_dimension=1, tiled=True)  73.2 us
    all_gather x1, waiting for transfers between devices, from_root(): return jnp.sum(lax.all_gather(kept, axis), axis=0)  49.6 us
    all_gather x1, blocking collectives, local(): x_col = lax.all_gather(vectors, 'row', axis=1, tiled=True)  25 us
    dot_general x1, matrix products, slot_terms(): normal = jnp.einsum('vsk,smk->vsm', picked_col, blocks, precision=HIGH)  15.5 us
    dot_general x1, matrix products, slot_terms(): transposed = jnp.einsum('vsm,smk->vsk', picked_row, blocks, precision=HIGH)  9.6 us
  transfers between devices with their start and end apart: 3, of which 3 were waited for; matrix products, arithmetic and copies ran while one was open for 10% of the time, Pallas kernels for 0%

profile of v2, /device:TPU:32, one launch (start us, length us, event | category | flops | bytes accessed | tf_op | source)
XLA Modules:
  0.0 320.1 jit_solution(3760047166257921980)
XLA Ops:
  6.5 0.0 all-gather.3.cloned.1.call-start
  6.5 25.0 %all_gather.9 = f32[16,2048]{1,0:T(8,128)S(1)} all-gather(f32[16,128]{1,0:T(8,128)} %param.6), channel_id=1, replica_groups=mesh['row'=16,'col'=16] {'row'}, dimensions={1}, use_global_device_ids=true | all-gather | bytes 139264 | tf_op jit(solution)/shard_map/all_gather | solution.py:51
  31.5 0.7 broadcast_select_fusion
  32.2 0.0 all-gather.3.cloned.1.call-update
  32.2 0.0 all-reduce.2.cloned.1.call-start
  32.9 0.7 compare_and_fusion
  33.6 0.8 gather_fusion.1
  34.4 15.5 %fusion.7 = f32[16,128,128]{2,0,1:T(8,128)S(1)} fusion(f32[1,1,128,128,128]{4,3,2,1,0:T(8,128)} %param.7, f32[128,16,128]{2,1,0:T(8,128)S(1)} %gather_fusion.1, pred[128]{0:T(512)(128)(4,1)S(1)} %get-tuple-element.6), kind=kOutput, calls=%fused_computation.7 | convolution fusion | flops 402915328 | bytes 10485888 | tf_op jit(solution)/shard_map/vsk,smk->vsm/dot_general | solution.py:23
  49.9 0.9 fusion.12
  50.8 0.7 copy.21
  51.5 0.0 all-reduce.2.cloned.1.call-update
  51.5 0.0 reduce-scatter.2.cloned.1.call-start
  51.6 49.6 %all-gather.3.cloned.1.call-done = f32[256,2048]{1,0:T(8,128)} async-done(((f32[16,2048]{1,0:T(8,128)}), f32[256,2048]{1,0:T(8,128)}) %all-gather.3.cloned.1.call-update) | async-done | bytes 2097168 | tf_op jit(solution)/shard_map/all_gather | solution.py:11
  101.2 1.7 reduce_sum.9
  102.9 0.8 gather_fusion
  103.7 9.6 %fusion.4 = f32[16,128,128]{2,0,1:T(8,128)S(1)} fusion(f32[1,1,128,128,128]{4,3,2,1,0:T(8,128)} %param.7, f32[128,16,128]{2,1,0:T(8,128)S(1)} %gather_fusion, pred[128]{0:T(512)(128)(4,1)S(1)} %get-tuple-element.10), kind=kOutput, calls=%fused_computation.6 | convolution fusion | flops 402915328 | bytes 10485888 | tf_op jit(solution)/shard_map/vsm,smk->vsk/dot_general | solution.py:24
  113.3 0.9 fusion.14
  114.2 124.6 %all-reduce.2.cloned.1.call-done = f32[16,2048]{1,0:T(8,128)} async-done(((f32[16,2048]{1,0:T(8,128)}), f32[16,2048]{1,0:T(8,128)}) %all-reduce.2.cloned.1.call-update) | async-done | bytes 131088 | tf_op jit(solution)/shard_map/psum | solution.py:55
  238.8 1.6 bitcast_add_fusion
  240.4 0.0 reduce-scatter.2.cloned.1.call-update
  240.4 73.2 %reduce-scatter.2.cloned.1.call-done = f32[16,128]{1,0:T(8,128)} async-done(((f32[16,2048]{1,0:T(8,128)}), f32[16,128]{1,0:T(8,128)}) %reduce-scatter.2.cloned.1.call-update) | async-done | bytes 8208 | tf_op jit(solution)/shard_map/reduce_scatter | solution.py:58
  (7 shorter events, 0.0 us)
Async XLA Ops:
  6.5 94.7 %all-gather.3.cloned.1.call-start = ((), (), s32[]{:S(2)}) async-start(), calls=%async_computation.3 | async-start | bytes 2228224 | tf_op jit(solution)/shard_map/all_gather | solution.py:11
  32.2 206.6 %all-reduce.2.cloned.1.call-start = ((), (), s32[]{:S(2)}) async-start(), calls=%async_computation.1 | async-start | bytes 262144 | tf_op jit(solution)/shard_map/psum | solution.py:55
  51.5 262.1 %reduce-scatter.2.cloned.1.call-start = ((), (), s32[]{:S(2)}) async-start(), calls=%async_computation.2 | async-start | bytes 139264 | tf_op jit(solution)/shard_map/reduce_scatter | solution.py:58
Sparse Core Ops, SparseCore 0:
  32.3 68.8 all-gather.2
  103.8 134.9 all-reduce.1
  242.7 70.8 reduce-scatter.1
